TPU v7x, 32 devices: a whole 2x2x4 slice. The times are simulated.
32 devices in a mesh: ty: 8 (over z, x), tx: 4 (over y, core).
Axes of the slice: x: 2, y: 2, z: 4, core: 2. Of those that a mesh axis runs over, the one named last changes fastest.
Arguments:
- specimen: float32 [2, 2048, 4096], P(None, 'ty', 'tx'), may hold values from -5 to 5
- probe_modes: float32 [4, 2, 128, 128], replicated, may hold values from -0.75 to 0.75
- patterns: float32 [256, 128, 128], P(('ty', 'tx')), may hold values from 0.25 to 2.5
- tile_row: int32 [256], P(('ty', 'tx')), may hold values from 0 to 7, as said below
- row_offset: int32 [256], P(('ty', 'tx')), may hold values from 0 to 128
- col_offset: int32 [256], P(('ty', 'tx')), may hold values from 0 to 896
Outputs:
- specimen_out: float32 [2, 2048, 4096], P(None, 'ty', 'tx')
- probe_out: float32 [4, 2, 128, 128], replicated
Inputs may be any that keep to these rules, and one draw needn't show every extreme that they name: `tile_row`: each index of ty+tx holds 8 consecutive positions. At most 2 of one device's positions name the same tile row, and for every index of tx some tile row is named exactly 2 times by each device with that tx index.
All inputs are finite; a program needn't handle non-finite values.
Results may differ from a plain program's by a relative error of at most 0.0001.
Values sent between devices are 32-bit elements; how exact they have to be, the bound alone decides.
A program may use at most 192 MiB of HBM per device.

v0:
```python
import math
import jax
import jax.numpy as jnp
from jax import lax
from jax.sharding import PartitionSpec as P

ITERS = 2
AMP_FLOOR = 0.3
OBJ_STEP = 1.0
SMALL_EPS = 1e-06
HIGHEST_PREC = lax.Precision.HIGHEST


def dft_tables(length):
    counter = jnp.arange(length, dtype=jnp.int32)
    product = counter[:, None] * counter[None, :] % length
    angles = product.astype(jnp.float32) * (2.0 * math.pi / length)
    norming = 1.0 / math.sqrt(length)
    return (jnp.cos(angles) * norming, jnp.sin(angles) * norming)


def left_apply(matrix, values):
    return jnp.einsum("kn,abnx->abkx", matrix, values, precision=HIGHEST_PREC)


def right_apply(values, matrix):
    return jnp.einsum("abxn,nl->abxl", values, matrix, precision=HIGHEST_PREC)


def transform(real_part, imag_part, cos_table, sin_table, direction):
    real_mid = left_apply(cos_table, real_part) - direction * left_apply(sin_table, imag_part)
    imag_mid = left_apply(cos_table, imag_part) + direction * left_apply(sin_table, real_part)
    real_out = right_apply(real_mid, cos_table) - direction * right_apply(imag_mid, sin_table)
    imag_out = right_apply(imag_mid, cos_table) + direction * right_apply(real_mid, sin_table)
    return (real_out, imag_out)


def position_terms(windows, probe_modes, intensity, weight, cos_table, sin_table):
    spec_real = windows[:, 0][:, None]
    spec_imag = windows[:, 1][:, None]
    mode_real = probe_modes[:, 0][None]
    mode_imag = probe_modes[:, 1][None]
    wave_real = mode_real * spec_real - mode_imag * spec_imag
    wave_imag = mode_real * spec_imag + mode_imag * spec_real
    far_real, far_imag = transform(wave_real, wave_imag, cos_table, sin_table, -1.0)
    model_power = jnp.sum(far_real * far_real + far_imag * far_imag, axis=1)
    factor = jnp.sqrt(intensity) / jnp.maximum(jnp.sqrt(model_power), AMP_FLOOR) - 1.0
    back_real, back_imag = transform(
        far_real * factor[:, None], far_imag * factor[:, None], cos_table, sin_table, 1.0
    )
    grad_real = jnp.sum(mode_real * back_real + mode_imag * back_imag, axis=1)
    grad_imag = jnp.sum(mode_real * back_imag - mode_imag * back_real, axis=1)
    weights = weight[:, None, None, None]
    modes_real = jnp.sum(weights * (spec_real * back_real + spec_imag * back_imag), axis=0)
    modes_imag = jnp.sum(weights * (spec_real * back_imag - spec_imag * back_real), axis=0)
    grad_window = jnp.stack([grad_real, grad_imag], axis=1) * weights
    grad_modes = jnp.stack([modes_real, modes_imag], axis=1)
    lighting = jnp.sum(weight[:, None, None] * (windows[:, 0] ** 2 + windows[:, 1] ** 2), axis=0)
    return (grad_window, grad_modes, lighting)


def cut_windows(tile_field, rows_at, cols_at, window):
    anchor = jnp.int32(0)

    def cut_one(row_at, col_at):
        return lax.dynamic_slice(tile_field, (anchor, row_at, col_at), (2, window, window))

    return jax.vmap(cut_one)(rows_at, cols_at)


def deposit_windows(tile_field, updates, rows_at, cols_at):
    anchor = jnp.int32(0)
    window = updates.shape[-1]

    def deposit(position, running_field):
        corner = (anchor, rows_at[position], cols_at[position])
        region = lax.dynamic_slice(running_field, corner, (2, window, window))
        return lax.dynamic_update_slice(running_field, region + updates[position], corner)

    return lax.fori_loop(0, updates.shape[0], deposit, tile_field)


def shards(specimen, probe_modes, patterns, tile_row, row_offset, col_offset):
    own_count = patterns.shape[0]
    window = patterns.shape[-1]
    grid_rows = lax.axis_size("ty")
    capacity = max(2, 2 * own_count // grid_rows)
    slots_all = grid_rows * capacity
    cos_table, sin_table = dft_tables(window)
    serial = jnp.arange(own_count, dtype=jnp.int32)
    same_row = tile_row[:, None] == tile_row[None, :]
    earlier = serial[None, :] < serial[:, None]
    rank_in_row = jnp.sum(jnp.logical_and(same_row, earlier), axis=1)
    slot_of = tile_row * capacity + rank_in_row
    request_rows = jnp.stack([row_offset, col_offset, jnp.ones_like(row_offset)], axis=1)
    requests = jnp.zeros((slots_all, 3), jnp.int32).at[slot_of].set(request_rows)
    request_grid = requests.reshape(grid_rows, capacity, 3)
    pattern_grid = jnp.zeros((slots_all, window, window), jnp.float32).at[slot_of].set(patterns)
    pattern_grid = pattern_grid.reshape(grid_rows, capacity, window, window)
    seen_grid, measured = (
        lax.all_to_all(request_grid, "ty", split_axis=0, concat_axis=0, tiled=True),
        lax.all_to_all(pattern_grid, "ty", split_axis=0, concat_axis=0, tiled=True),
    )
    seen_flat = seen_grid.reshape(slots_all, 3)
    measured = measured.reshape(slots_all, window, window)
    valid = seen_flat[:, 2].astype(jnp.float32)
    for sweep_index in range(ITERS):
        probe_power = jnp.sum(probe_modes[:, 0] ** 2 + probe_modes[:, 1] ** 2, axis=0)
        obj_scale = OBJ_STEP / (jnp.max(probe_power) + SMALL_EPS)
        windows = cut_windows(specimen, seen_flat[:, 0], seen_flat[:, 1], window)
        grad_window, grad_modes, lighting = position_terms(
            windows, probe_modes, measured, valid, cos_table, sin_table
        )
        specimen = deposit_windows(
            specimen, obj_scale * grad_window, seen_flat[:, 0], seen_flat[:, 1]
        )
        grad_total, light_total = lax.psum((grad_modes, lighting), ("ty", "tx"))
        probe_modes = probe_modes + grad_total / (jnp.max(light_total) + SMALL_EPS)
    return (specimen, probe_modes)


def solution(mesh):
    placed = (
        P(None, "ty", "tx"),
        P(),
        P(("ty", "tx"), None, None),
        P(("ty", "tx")),
        P(("ty", "tx")),
        P(("ty", "tx")),
    )
    return jax.shard_map(
        shards, mesh=mesh, in_specs=placed, out_specs=(P(None, "ty", "tx"), P()), check_vma=False
    )
```

profile of v0, /device:TPU:3, one launch (start us, length us, event | category | flops | bytes accessed | tf_op | source)
XLA Modules:
  0.0 804.8 jit_solution(782398883551330315)
XLA Ops:
  9.5 5.8 all-to-all-start
  16.5 2.7 scatter_fusion
  20.5 5.5 all-to-all-start.1
  26.3 42.8 %while.30 = (s32[]{:T(128)}, f32[2,256,1024]{2,1,0:T(8,128)S(1)}, s32[16,3]{0,1:T(4,128)S(1)}, f32[16,2,128,128]{3,2,0,1:T(8,128)}, s32[]{:T(128)}) while((s32[]{:T(128)}, f32[2,256,1024]{2,1,0:T(8,128)S(1)}, s32[16,3]{0,1:T(4,128)S(1)}, f32[16,2,128,128]{3,2,0,1:T(8,128)}, s32[]{:T(128)}) %tuple.120), condition=%wide.while_cond, body=%wide.while_body.sunk | while | flops 2 | bytes 263785 | solution.py:66
  72.1 7.3 fusion.36
  79.4 7.4 multiply_add_fusion.6
  86.8 8.7 %fusion.26 = f32[16,4,128,128]{3,2,1,0:T(8,128)} fusion(f32[16,4,128,128]{3,2,1,0:T(8,128)S(1)} %multiply_add_fusion.6), kind=kOutput, calls=%fused_computation.34 | convolution fusion | flops 1610858496 | bytes 8388608 | tf_op jit(solution)/shard_map/abxn,nl->abxl/dot_general | solution.py:27
  95.5 8.7 %fusion.24 = f32[16,4,128,128]{3,2,1,0:T(8,128)} fusion(f32[16,4,128,128]{3,2,1,0:T(8,128)S(1)} %multiply_add_fusion.6), kind=kOutput, calls=%fused_computation.32 | convolution fusion | flops 1610858496 | bytes 8388608 | tf_op jit(solution)/shard_map/abxn,nl->abxl/dot_general | solution.py:27
  104.2 9.0 %fusion.37 = f32[16,4,128,128]{3,2,1,0:T(8,128)} fusion(f32[16,128,128]{2,1,0:T(8,128)S(1)} %get-tuple-element.267, f32[4,128,128]{2,1,0:T(8,128)S(1)} %get-tuple-element.271, f32[16,128,128]{2,1,0:T(8,128)S(1)} %get-tuple-element.266, f32[4,128,128]{2,1,0:T(8,128)S(1)} %get-tuple-element.270), kind=kOutput, calls=%fused_computation.66 | convolution fusion | flops 1614004224 | bytes 6815744 | tf_op jit(solution)/shard_map/kn,abnx->abkx/dot_general | solution.py:23
  113.2 9.4 %multiply_subtract_fusion.6 = f32[16,4,128,128]{3,2,1,0:T(8,128)S(1)} fusion(f32[16,4,128,128]{3,2,1,0:T(8,128)} %fusion.37, f32[16,128,128]{2,1,0:T(8,128)S(1)} %get-tuple-element.267, f32[4,128,128]{2,1,0:T(8,128)S(1)} %get-tuple-element.271, f32[16,128,128]{2,1,0:T(8,128)S(1)} %get-tuple-element.266, f32[4,128,128]{2,1,0:T(8,128)S(1)} %get-tuple-element.270), kind=kOutput, calls=%fused_computation.63 | convolution fusion | flops 1616101376 | bytes 11010048 | tf_op jit(solution)/shard_map/kn,abnx->abkx/dot_general | solution.py:23
  122.7 6.9 multiply_subtract_fusion.5
  131.5 10.3 %add_reduce_fusion.3 = (f32[16,128,128]{2,1,0:T(8,128)}, f32[16,4,128,128]{3,2,1,0:T(8,128)}) fusion(f32[16,4,128,128]{3,2,1,0:T(8,128)S(1)} %multiply_subtract_fusion.5, f32[16,4,128,128]{3,2,1,0:T(8,128)S(1)} %copy-done.4, f32[16,4,128,128]{3,2,1,0:T(8,128)S(1)} %multiply_subtract_fusion.6), kind=kOutput, calls=%fused_computation.59 | convolution fusion | flops 1616887808 | bytes 17825792 | tf_op jit(solution)/shard_map/abxn,nl->abxl/dot_general | solution.py:27
  145.2 6.9 fusion.50
  152.1 7.3 fusion.48
  159.3 6.8 fusion.79
  166.2 7.3 fusion.18
  173.5 7.3 fusion.16
  180.7 7.1 fusion.76
  187.9 7.3 fusion.60
  195.2 11.2 %multiply_reduce_fusion.3 = (f32[4,128,128]{2,1,0:T(8,128)}, f32[4,128,128]{2,1,0:T(8,128)}, f32[16,128,128]{2,1,0:T(8,128)S(1)}, f32[16,128,128]{2,1,0:T(8,128)S(1)}) fusion(f32[16,4,128,128]{3,2,1,0:T(8,128)S(1)} %fusion.60, f32[16]{0:T(128)S(1)} %bitcast.253, f32[16,128,128]{2,1,0:T(8,128)S(1)} %get-tuple-element.267, ...), kind=kOutput, calls=%fused_computation.56 | convolution fusion | flops 1630126080 | bytes 17825856 | tf_op jit(solution)/shard_map/abxn,nl->abxl/dot_general | solution.py:27
  208.8 135.7 %while.28 = (s32[]{:T(128)}, f32[2,256,1024]{2,1,0:T(8,128)S(1)}, s32[16]{0:T(128)S(1)}, s32[16]{0:T(128)S(1)}, f32[16,2,128,128]{3,2,1,0:T(8,128)}, /*index=5*/s32[]{:T(128)}, s32[]{:T(128)}, s32[]{:T(128)}, s32[]{:T(128)}) while((s32[]{:T(128)}, f32[2,256,1024]{2,1,0:T(8,128)S(1)}, s32[16]{0:T(128)S(1)}, s32[16]{0:T(128)S(1)}, ...), condition=%wide.region_9.10_spmd, body=%wide.region_8.9_spmd.sunk | while | flops 32776 | bytes 655561 | solution.py:80
  223.1 2.5 dynamic_update_slice.16
  240.2 2.3 dynamic_update_slice.16
  248.6 2.4 dynamic_update_slice.16
  257.2 2.4 dynamic_update_slice.16
  265.7 2.4 dynamic_update_slice.16
  274.3 2.4 dynamic_update_slice.16
  282.8 2.3 dynamic_update_slice.16
  291.3 2.4 dynamic_update_slice.16
  308.2 2.5 dynamic_update_slice.16
  325.2 2.3 dynamic_update_slice.16
  333.6 2.4 dynamic_update_slice.16
  344.4 42.9 %while.31 = (s32[]{:T(128)}, f32[2,256,1024]{2,1,0:T(8,128)S(1)}, s32[16,3]{0,1:T(4,128)S(1)}, f32[16,2,128,128]{3,2,1,0:T(8,128)}, s32[]{:T(128)}) while((s32[]{:T(128)}, f32[2,256,1024]{2,1,0:T(8,128)S(1)}, s32[16,3]{0,1:T(4,128)S(1)}, f32[16,2,128,128]{3,2,1,0:T(8,128)}, s32[]{:T(128)}) %tuple.121), condition=%wide.while_cond.1, body=%wide.while_body.1.sunk | while | flops 2 | bytes 263785 | solution.py:66
  387.3 4.1 multiply_reduce_fusion.4
  395.1 127.0 %all-reduce.7.cloned.1.call-done = (f32[4,2,128,128]{3,2,1,0:T(8,128)}, f32[128,128]{1,0:T(8,128)}) async-done(((f32[4,2,128,128]{3,2,1,0:T(8,128)}, f32[128,128]{1,0:T(8,128)}), (f32[4,2,128,128]{3,2,1,0:T(8,128)}, f32[128,128]{1,0:T(8,128)})) %all-reduce.7.cloned.1.call-update) | async-done | bytes 589840 | tf_op jit(solution)/shard_map/psum | solution.py:117
  525.5 7.2 fusion.33
  532.7 7.6 fusion.32
  540.3 7.3 multiply_add_fusion.1
  547.6 7.5 fusion.10
  555.0 7.2 fusion.8
  562.3 7.4 multiply_subtract_fusion.1
  569.7 7.1 multiply_subtract_fusion
  576.8 7.1 add_reduce_fusion.1
  584.3 7.6 fusion.42
  591.9 7.1 fusion.40
  599.0 7.4 fusion.85
  606.4 9.5 %fusion.2 = f32[16,4,128,128]{3,2,1,0:T(8,128)} fusion(f32[16,4,128,128]{3,2,1,0:T(8,128)S(1)} %fusion.85), kind=kOutput, calls=%fused_computation.10 | convolution fusion | flops 1610858496 | bytes 8388608 | tf_op jit(solution)/shard_map/abxn,nl->abxl/dot_general | solution.py:27
  615.9 8.6 %fusion = f32[16,4,128,128]{3,2,1,0:T(8,128)} fusion(f32[16,4,128,128]{3,2,1,0:T(8,128)S(1)} %fusion.85), kind=kOutput, calls=%fused_computation.8 | convolution fusion | flops 1610858496 | bytes 8388608 | tf_op jit(solution)/shard_map/abxn,nl->abxl/dot_general | solution.py:27
  624.6 8.6 %fusion.82 = f32[16,4,128,128]{3,2,1,0:T(8,128)} fusion(f32[16,4,128,128]{3,2,1,0:T(8,128)S(1)} %fusion.42, f32[16,4,128,128]{3,2,1,0:T(8,128)S(1)} %multiply_subtract_fusion, f32[16,128,128]{2,1,0:T(8,128)S(1)} %fusion.131), kind=kOutput, calls=%fused_computation.92 | convolution fusion | flops 1612955648 | bytes 13631488 | tf_op jit(solution)/shard_map/kn,abnx->abkx/dot_general | solution.py:23
  634.6 10.0 %fusion.70 = f32[16,4,128,128]{3,2,1,0:T(8,128)S(1)} fusion(f32[16,4,128,128]{3,2,1,0:T(8,128)} %fusion.2, f32[16,4,128,128]{3,2,1,0:T(8,128)} %fusion.82), kind=kOutput, calls=%fused_computation.88 | convolution fusion | flops 1611907072 | bytes 12582912 | tf_op jit(solution)/shard_map/abxn,nl->abxl/dot_general | solution.py:27
  644.6 11.7 %multiply_reduce_fusion.1 = (f32[4,128,128]{2,1,0:T(8,128)S(1)}, f32[4,128,128]{2,1,0:T(8,128)S(1)}, f32[16,128,128]{2,1,0:T(8,128)}, f32[16,128,128]{2,1,0:T(8,128)}) fusion(f32[16,4,128,128]{3,2,1,0:T(8,128)S(1)} %fusion.70, f32[16,128,128]{2,1,0:T(8,128)S(1)} %slice_bitcast_fusion, f32[16,128,128]{2,1,0:T(8,128)S(1)} %slice_bitcast_fusion.1, ...), kind=kOutput, calls=%fused_computation.41 | convolution fusion | flops 1630126080 | bytes 17825856 | tf_op jit(solution)/shard_map/abxn,nl->abxl/dot_general | solution.py:27
  657.2 3.3 fusion.89
  660.5 132.9 %while.29 = (s32[]{:T(128)}, f32[2,256,1024]{2,1,0:T(8,128)S(1)}, s32[16]{0:T(128)S(1)}, s32[16]{0:T(128)S(1)}, f32[16,2,128,128]{3,2,1,0:T(8,128)}, /*index=5*/s32[]{:T(128)}, s32[]{:T(128)}, s32[]{:T(128)}, s32[]{:T(128)}) while((s32[]{:T(128)}, f32[2,256,1024]{2,1,0:T(8,128)S(1)}, s32[16]{0:T(128)S(1)}, s32[16]{0:T(128)S(1)}, ...), condition=%wide.region_22.23_spmd, body=%wide.region_21.22_spmd.sunk | while | flops 32776 | bytes 655561 | solution.py:80
  674.5 2.5 dynamic_update_slice.17
  691.2 2.3 dynamic_update_slice.17
  699.5 2.4 dynamic_update_slice.17
  707.9 2.4 dynamic_update_slice.17
  716.2 2.4 dynamic_update_slice.17
  724.6 2.4 dynamic_update_slice.17
  733.0 2.3 dynamic_update_slice.17
  741.3 2.4 dynamic_update_slice.17
  757.9 2.5 dynamic_update_slice.17
  774.5 2.3 dynamic_update_slice.17
  782.7 2.4 dynamic_update_slice.17
  (294 shorter events, 206.9 us)
Async XLA Ops:
  7.2 8.1 %copy-start.18 = (f32[4,2,128,128]{3,2,1,0:T(8,128)S(1)}, f32[4,2,128,128]{3,2,1,0:T(8,128)}, u32[]{:S(2)}) copy-start(f32[4,2,128,128]{3,2,1,0:T(8,128)} %param.11) | copy-start | bytes 1572868
  7.2 0.7 copy-start.24
  7.2 1.0 copy-start.23
  7.2 1.0 copy-start.22
  7.9 18.4 %copy-start.11 = (f32[2,256,1024]{2,1,0:T(8,128)S(1)}, f32[2,256,1024]{2,1,0:T(8,128)}, u32[]{:S(2)}) copy-start(f32[2,256,1024]{2,1,0:T(8,128)} %param.10) | copy-start | bytes 6291460
  9.5 11.1 %all-to-all-start = ((s32[8,2,3]{2,1,0:T(2,128)}), s32[8,2,3]{2,1,0:T(2,128)S(1)}, u32[]{:S(2)}, u32[]{:S(2)}) async-start(s32[8,2,3]{2,1,0:T(2,128)} %bitcast.8), calls=%async_computation | async-start | bytes 16384 | tf_op jit(solution)/shard_map/all_to_all | solution.py:101
  15.3 97.9 %copy-start.14 = (f32[4,128,128]{2,1,0:T(8,128)}, f32[4,128,128]{2,1,0:T(8,128)S(1)}, u32[]{:S(2)}) copy-start(f32[4,128,128]{2,1,0:T(8,128)S(1)} %get-tuple-element.271) | copy-start | bytes 786436
  20.5 121.3 %all-to-all-start.1 = ((f32[8,2,128,128]{3,2,1,0:T(8,128)}), f32[8,2,128,128]{3,2,1,0:T(8,128)}, u32[]{:S(2)}, u32[]{:S(2)}) async-start(f32[8,2,128,128]{3,2,1,0:T(8,128)} %bitcast.24), calls=%async_computation.1 | async-start | bytes 2097152 | tf_op jit(solution)/shard_map/all_to_all | solution.py:102
  26.0 496.1 %all-reduce.7.cloned.1.call-start = ((), (), s32[]{:S(2)}) async-start(), calls=%async_computation.3 | async-start | bytes 1179648 | tf_op jit(solution)/shard_map/psum | solution.py:117
  69.0 1.3 copy-start.6
  113.2 9.4 %copy-start.5 = (f32[16,4,128,128]{3,2,1,0:T(8,128)S(1)}, f32[16,4,128,128]{3,2,1,0:T(8,128)}, u32[]{:S(2)}) copy-start(f32[16,4,128,128]{3,2,1,0:T(8,128)} %fusion.26) | copy-start | bytes 12582916
  122.7 8.9 %copy-start.4 = (f32[16,4,128,128]{3,2,1,0:T(8,128)S(1)}, f32[16,4,128,128]{3,2,1,0:T(8,128)}, u32[]{:S(2)}) copy-start(f32[16,4,128,128]{3,2,1,0:T(8,128)} %fusion.24) | copy-start | bytes 12582916
  129.6 1.9 copy-start
  141.9 3.3 copy-start.2
  152.0 7.3 copy-start.1
  187.9 7.3 copy-start.15
  206.4 2.3 copy-start.7
  208.8 182.6 %copy-start.20 = (f32[4,128,128]{2,1,0:T(8,128)S(1)}, f32[4,128,128]{2,1,0:T(8,128)}, u32[]{:S(2)}) copy-start(f32[4,128,128]{2,1,0:T(8,128)} %get-tuple-element.210) | copy-start | bytes 786436
  387.3 5.0 copy-start.8
  387.3 4.1 copy-start.21
  392.3 401.1 %all-reduce.5.cloned.1.call-start = ((), (), s32[]{:S(2)}) async-start(), calls=%async_computation.2 | async-start | bytes 1179648 | tf_op jit(solution)/shard_map/psum | solution.py:117
  525.5 99.1 %copy-start.12 = (f32[4,2,128,128]{3,2,1,0:T(8,128)}, f32[4,2,128,128]{3,2,1,0:T(8,128)S(1)}, u32[]{:S(2)}) copy-start(f32[4,2,128,128]{3,2,1,0:T(8,128)S(1)} %divide_add_fusion.1) | copy-start | bytes 1572868
  525.5 36.7 %copy-start.16 = (f32[4,128,128]{2,1,0:T(8,128)}, f32[4,128,128]{2,1,0:T(8,128)S(1)}, u32[]{:S(2)}) copy-start(f32[4,128,128]{2,1,0:T(8,128)S(1)} %get-tuple-element.269) | copy-start | bytes 786436
  634.5 10.1 %copy-start.3 = (f32[16,4,128,128]{3,2,1,0:T(8,128)S(1)}, f32[16,4,128,128]{3,2,1,0:T(8,128)}, u32[]{:S(2)}) copy-start(f32[16,4,128,128]{3,2,1,0:T(8,128)} %fusion.82) | copy-start | bytes 12582916
  634.5 10.1 %copy-start.17 = (f32[4,128,128]{2,1,0:T(8,128)S(1)}, f32[4,128,128]{2,1,0:T(8,128)}, u32[]{:S(2)}) copy-start(f32[4,128,128]{2,1,0:T(8,128)} %copy-done.16) | copy-start | bytes 786436
  634.6 10.1 %copy-start.19 = (f32[16,4,128,128]{3,2,1,0:T(8,128)S(1)}, f32[16,4,128,128]{3,2,1,0:T(8,128)}, u32[]{:S(2)}) copy-start(f32[16,4,128,128]{3,2,1,0:T(8,128)} %fusion) | copy-start | bytes 12582916
  656.3 4.2 copy-start.9
  657.1 138.4 %copy-start.13 = (f32[4,2,128,128]{3,2,1,0:T(8,128)S(1)}, f32[4,2,128,128]{3,2,1,0:T(8,128)}, u32[]{:S(2)}) copy-start(f32[4,2,128,128]{3,2,1,0:T(8,128)} %copy-done.12) | copy-start | bytes 1572868
  793.4 4.1 copy-start.10
Sparse Core Ops, SparseCore 0:
  392.4 129.6 all-reduce.6
  657.3 129.1 all-reduce.4
where the time goes:
time: 817 us; the launch traced here: 805 us
  matrix products  258 us (32%)
  local copies, waits for them, and re-layouts  216 us (26%)
  waiting for transfers between devices  127 us (16%)
  loops' own time  122 us (15%)
  other arithmetic  53.2 us (7%)
  between operations  17.6 us (2%)
  starting transfers between devices  11.5 us (1%)
    dot_general x16, matrix products, right_apply(): return jnp.einsum('abxn,nl->abxl', values, matrix, precision=HIGHEST_PREC)  136 us
    psum x2, waiting for transfers between devices, shards(): grad_total, light_total = lax.psum((grad_modes, lighting), ('ty', 'tx'))  127 us
    another operation x2, loops' own time, deposit_windows(): return lax.fori_loop(0, updates.shape[0], deposit, tile_field)  122 us
    dot_general x16, matrix products, left_apply(): return jnp.einsum('kn,abnx->abkx', matrix, values, precision=HIGHEST_PREC)  121 us
    gather x96, local copies, waits for them, and re-layouts  85.6 us
    dynamic_update_slice x32, local copies, waits for them, and re-layouts, deposit(): lax.dynamic_update_slice(running_field, region + updates[position], corner)  74.4 us
    dynamic_slice x64, local copies, waits for them, and re-layouts, deposit(): corner = (anchor, rows_at[position], cols_at[position])  40 us
    add x32, other arithmetic, deposit(): region + updates[position]  32.6 us
  transfers between devices with their start and end apart: 4, of which 1 were waited for; matrix products, arithmetic and copies ran while one was open for 24% of the time, Pallas kernels for 0%

commit v1 on v0

--- a/solution.py
+++ b/solution.py
@@ -114,7 +114,7 @@
         specimen = deposit_windows(
             specimen, obj_scale * grad_window, seen_flat[:, 0], seen_flat[:, 1]
         )
-        grad_total, light_total = lax.psum((grad_modes, lighting), ("ty", "tx"))
+        grad_total, light_total = lax.psum(lax.psum((grad_modes, lighting), "tx"), "ty")
         probe_modes = probe_modes + grad_total / (jnp.max(light_total) + SMALL_EPS)
     return (specimen, probe_modes)
 

time: 817 us -> 821 us (level)
  waiting for transfers between devices: 127 us -> 136 us
    psum x2 -> x4, waiting for transfers between devices: 127 us -> 136 us  [the longest x2 72.2 us: shards(): lax.psum(lax.psum((grad_modes, lighting), 'tx'), 'ty')]
  transfers between devices with their start and end apart: 4 -> 6, of which waited for: 1 -> 3; matrix products, arithmetic and copies ran while one was open for 24% -> 24% of each run, Pallas kernels for 0% -> 0%
where the time goes in v1:
time: 821 us; the launch traced here: 808 us
  matrix products  250 us (30%)
  local copies, waits for them, and re-layouts  216 us (26%)
  waiting for transfers between devices  136 us (17%)
  loops' own time  124 us (15%)
  other arithmetic  53.1 us (6%)
  between operations  17.1 us (2%)
  starting transfers between devices  11.6 us (1%)
    dot_general x16, matrix products, right_apply(): return jnp.einsum('abxn,nl->abxl', values, matrix, precision=HIGHEST_PREC)  130 us
    another operation x2, loops' own time, deposit_windows(): return lax.fori_loop(0, updates.shape[0], deposit, tile_field)  124 us
    dot_general x16, matrix products, left_apply(): return jnp.einsum('kn,abnx->abkx', matrix, values, precision=HIGHEST_PREC)  120 us
    gather x96, local copies, waits for them, and re-layouts  85.6 us
    dynamic_update_slice x32, local copies, waits for them, and re-layouts, deposit(): lax.dynamic_update_slice(running_field, region + updates[position], corner)  74.4 us
    psum x2, waiting for transfers between devices, shards(): lax.psum(lax.psum((grad_modes, lighting), 'tx'), 'ty')  72.2 us
    psum x2, waiting for transfers between devices, shards(): lax.psum((grad_modes, lighting), 'tx')  63.5 us
    dynamic_slice x64, local copies, waits for them, and re-layouts, deposit(): corner = (anchor, rows_at[position], cols_at[position])  39.6 us
  transfers between devices with their start and end apart: 6, of which 3 were waited for; matrix products, arithmetic and copies ran while one was open for 24% of the time, Pallas kernels for 0%

profile of v1, /device:TPU:3, one launch (start us, length us, event | category | flops | bytes accessed | tf_op | source)
XLA Modules:
  0.0 808.0 jit_solution(12860135443059371960)
XLA Ops:
  9.5 5.8 all-to-all-start
  16.5 2.7 scatter_fusion
  20.5 5.5 all-to-all-start.1
  26.3 42.8 %while.30 = (s32[]{:T(128)}, f32[2,256,1024]{2,1,0:T(8,128)S(1)}, s32[16,3]{0,1:T(4,128)S(1)}, f32[16,2,128,128]{3,2,0,1:T(8,128)}, s32[]{:T(128)}) while((s32[]{:T(128)}, f32[2,256,1024]{2,1,0:T(8,128)S(1)}, s32[16,3]{0,1:T(4,128)S(1)}, f32[16,2,128,128]{3,2,0,1:T(8,128)}, s32[]{:T(128)}) %tuple.126), condition=%wide.while_cond, body=%wide.while_body.sunk | while | flops 2 | bytes 263785 | solution.py:66
  72.1 7.3 fusion.36
  79.4 7.7 multiply_add_fusion.6
  87.0 8.7 %fusion.26 = f32[16,4,128,128]{3,2,1,0:T(8,128)} fusion(f32[16,4,128,128]{3,2,1,0:T(8,128)S(1)} %multiply_add_fusion.6), kind=kOutput, calls=%fused_computation.34 | convolution fusion | flops 1610858496 | bytes 8388608 | tf_op jit(solution)/shard_map/abxn,nl->abxl/dot_general | solution.py:27
  95.7 8.7 %fusion.24 = f32[16,4,128,128]{3,2,1,0:T(8,128)} fusion(f32[16,4,128,128]{3,2,1,0:T(8,128)S(1)} %multiply_add_fusion.6), kind=kOutput, calls=%fused_computation.32 | convolution fusion | flops 1610858496 | bytes 8388608 | tf_op jit(solution)/shard_map/abxn,nl->abxl/dot_general | solution.py:27
  104.4 8.7 %fusion.37 = f32[16,4,128,128]{3,2,1,0:T(8,128)} fusion(f32[16,128,128]{2,1,0:T(8,128)S(1)} %get-tuple-element.271, f32[4,128,128]{2,1,0:T(8,128)S(1)} %get-tuple-element.275, f32[16,128,128]{2,1,0:T(8,128)S(1)} %get-tuple-element.270, f32[4,128,128]{2,1,0:T(8,128)S(1)} %get-tuple-element.274), kind=kOutput, calls=%fused_computation.66 | convolution fusion | flops 1614004224 | bytes 6815744 | tf_op jit(solution)/shard_map/kn,abnx->abkx/dot_general | solution.py:23
  113.3 9.4 %multiply_subtract_fusion.6 = f32[16,4,128,128]{3,2,1,0:T(8,128)S(1)} fusion(f32[16,4,128,128]{3,2,1,0:T(8,128)} %fusion.37, f32[16,128,128]{2,1,0:T(8,128)S(1)} %get-tuple-element.271, f32[4,128,128]{2,1,0:T(8,128)S(1)} %get-tuple-element.275, f32[16,128,128]{2,1,0:T(8,128)S(1)} %get-tuple-element.270, f32[4,128,128]{2,1,0:T(8,128)S(1)} %get-tuple-element.274), kind=kOutput, calls=%fused_computation.63 | convolution fusion | flops 1616101376 | bytes 11010048 | tf_op jit(solution)/shard_map/kn,abnx->abkx/dot_general | solution.py:23
  122.7 6.9 multiply_subtract_fusion.5
  131.6 10.5 %add_reduce_fusion.3 = (f32[16,128,128]{2,1,0:T(8,128)}, f32[16,4,128,128]{3,2,1,0:T(8,128)}) fusion(f32[16,4,128,128]{3,2,1,0:T(8,128)S(1)} %multiply_subtract_fusion.5, f32[16,4,128,128]{3,2,1,0:T(8,128)S(1)} %copy-done.3, f32[16,4,128,128]{3,2,1,0:T(8,128)S(1)} %multiply_subtract_fusion.6), kind=kOutput, calls=%fused_computation.59 | convolution fusion | flops 1616887808 | bytes 17825792 | tf_op jit(solution)/shard_map/abxn,nl->abxl/dot_general | solution.py:27
  145.4 6.9 fusion.50
  152.3 7.0 fusion.48
  159.4 6.8 fusion.79
  166.2 7.3 fusion.18
  173.5 7.5 fusion.16
  181.0 7.1 fusion.76
  188.2 7.0 fusion.60
  195.2 11.2 %multiply_reduce_fusion.3 = (f32[4,128,128]{2,1,0:T(8,128)}, f32[4,128,128]{2,1,0:T(8,128)}, f32[16,128,128]{2,1,0:T(8,128)S(1)}, f32[16,128,128]{2,1,0:T(8,128)S(1)}) fusion(f32[16,4,128,128]{3,2,1,0:T(8,128)S(1)} %fusion.60, f32[16]{0:T(128)S(1)} %bitcast.253, f32[16,128,128]{2,1,0:T(8,128)S(1)} %get-tuple-element.271, ...), kind=kOutput, calls=%fused_computation.56 | convolution fusion | flops 1630126080 | bytes 17825856 | tf_op jit(solution)/shard_map/abxn,nl->abxl/dot_general | solution.py:27
  208.8 135.7 %while.28 = (s32[]{:T(128)}, f32[2,256,1024]{2,1,0:T(8,128)S(1)}, s32[16]{0:T(128)S(1)}, s32[16]{0:T(128)S(1)}, f32[16,2,128,128]{3,2,1,0:T(8,128)}, /*index=5*/s32[]{:T(128)}, s32[]{:T(128)}, s32[]{:T(128)}, s32[]{:T(128)}) while((s32[]{:T(128)}, f32[2,256,1024]{2,1,0:T(8,128)S(1)}, s32[16]{0:T(128)S(1)}, s32[16]{0:T(128)S(1)}, ...), condition=%wide.region_9.10_spmd, body=%wide.region_8.9_spmd.sunk | while | flops 32776 | bytes 655561 | solution.py:80
  223.2 2.5 dynamic_update_slice.16
  240.2 2.3 dynamic_update_slice.16
  248.7 2.4 dynamic_update_slice.16
  257.2 2.4 dynamic_update_slice.16
  265.8 2.4 dynamic_update_slice.16
  274.3 2.4 dynamic_update_slice.16
  282.8 2.3 dynamic_update_slice.16
  291.3 2.4 dynamic_update_slice.16
  308.2 2.5 dynamic_update_slice.16
  325.2 2.3 dynamic_update_slice.16
  333.6 2.4 dynamic_update_slice.16
  344.4 42.9 %while.31 = (s32[]{:T(128)}, f32[2,256,1024]{2,1,0:T(8,128)S(1)}, s32[16,3]{0,1:T(4,128)S(1)}, f32[16,2,128,128]{3,2,1,0:T(8,128)}, s32[]{:T(128)}) while((s32[]{:T(128)}, f32[2,256,1024]{2,1,0:T(8,128)S(1)}, s32[16,3]{0,1:T(4,128)S(1)}, f32[16,2,128,128]{3,2,1,0:T(8,128)}, s32[]{:T(128)}) %tuple.127), condition=%wide.while_cond.1, body=%wide.while_body.1.sunk | while | flops 2 | bytes 263785 | solution.py:66
  387.3 4.1 multiply_reduce_fusion.4
  392.3 33.5 %all-reduce.15.cloned.1.call-done = (f32[4,2,128,128]{3,2,1,0:T(8,128)}, f32[128,128]{1,0:T(8,128)}) async-done(((f32[4,2,128,128]{3,2,1,0:T(8,128)}, f32[128,128]{1,0:T(8,128)}), (f32[4,2,128,128]{3,2,1,0:T(8,128)}, f32[128,128]{1,0:T(8,128)})) %all-reduce.15.cloned.1.call-update) | async-done | bytes 589840 | tf_op jit(solution)/shard_map/psum | solution.py:117
  428.7 72.2 %all-reduce.11.cloned.1.call-done = (f32[4,2,128,128]{3,2,1,0:T(8,128)}, f32[128,128]{1,0:T(8,128)}) async-done(((f32[4,2,128,128]{3,2,1,0:T(8,128)}, f32[128,128]{1,0:T(8,128)}), (f32[4,2,128,128]{3,2,1,0:T(8,128)}, f32[128,128]{1,0:T(8,128)})) %all-reduce.11.cloned.1.call-update) | async-done | bytes 589840 | tf_op jit(solution)/shard_map/psum | solution.py:117
  505.1 7.2 fusion.33
  512.3 7.8 fusion.32
  520.1 7.3 multiply_add_fusion.1
  527.4 7.2 fusion.10
  534.7 7.3 fusion.8
  541.9 7.4 multiply_subtract_fusion.1
  549.4 7.3 multiply_subtract_fusion
  556.7 7.1 add_reduce_fusion.1
  564.2 7.3 fusion.42
  571.5 7.1 fusion.40
  578.7 7.4 fusion.85
  586.1 7.2 fusion.2
  593.4 6.9 fusion
  600.2 7.4 fusion.82
  607.6 6.9 fusion.70
  614.5 12.0 %multiply_reduce_fusion.1 = (f32[4,128,128]{2,1,0:T(8,128)S(1)}, f32[4,128,128]{2,1,0:T(8,128)S(1)}, f32[16,128,128]{2,1,0:T(8,128)}, f32[16,128,128]{2,1,0:T(8,128)}) fusion(f32[16,4,128,128]{3,2,1,0:T(8,128)S(1)} %fusion.70, f32[16,128,128]{2,1,0:T(8,128)S(1)} %slice_bitcast_fusion, f32[16,128,128]{2,1,0:T(8,128)S(1)} %slice_bitcast_fusion.1, ...), kind=kOutput, calls=%fused_computation.41 | convolution fusion | flops 1630126080 | bytes 17825856 | tf_op jit(solution)/shard_map/abxn,nl->abxl/dot_general | solution.py:27
  628.8 3.2 fusion.89
  632.0 30.1 %all-reduce.13.cloned.1.call-done = (f32[4,2,128,128]{3,2,1,0:T(8,128)}, f32[128,128]{1,0:T(8,128)}) async-done(((f32[4,2,128,128]{3,2,1,0:T(8,128)}, f32[128,128]{1,0:T(8,128)}), (f32[4,2,128,128]{3,2,1,0:T(8,128)}, f32[128,128]{1,0:T(8,128)})) %all-reduce.13.cloned.1.call-update) | async-done | bytes 589840 | tf_op jit(solution)/shard_map/psum | solution.py:117
  662.1 135.0 %while.29 = (s32[]{:T(128)}, f32[2,256,1024]{2,1,0:T(8,128)S(1)}, s32[16]{0:T(128)S(1)}, s32[16]{0:T(128)S(1)}, f32[16,2,128,128]{3,2,1,0:T(8,128)}, /*index=5*/s32[]{:T(128)}, s32[]{:T(128)}, s32[]{:T(128)}, s32[]{:T(128)}) while((s32[]{:T(128)}, f32[2,256,1024]{2,1,0:T(8,128)S(1)}, s32[16]{0:T(128)S(1)}, s32[16]{0:T(128)S(1)}, ...), condition=%wide.region_24.25_spmd, body=%wide.region_23.24_spmd.sunk | while | flops 32776 | bytes 655561 | solution.py:80
  676.4 2.5 dynamic_update_slice.17
  701.8 2.4 dynamic_update_slice.17
  710.3 2.4 dynamic_update_slice.17
  718.8 2.4 dynamic_update_slice.17
  727.3 2.4 dynamic_update_slice.17
  735.8 2.3 dynamic_update_slice.17
  744.3 2.4 dynamic_update_slice.17
  761.1 2.5 dynamic_update_slice.17
  786.3 2.4 dynamic_update_slice.17
  (292 shorter events, 212.0 us)
Async XLA Ops:
  7.2 8.1 %copy-start.15 = (f32[4,2,128,128]{3,2,1,0:T(8,128)S(1)}, f32[4,2,128,128]{3,2,1,0:T(8,128)}, u32[]{:S(2)}) copy-start(f32[4,2,128,128]{3,2,1,0:T(8,128)} %param.11) | copy-start | bytes 1572868
  7.2 0.7 copy-start.20
  7.2 1.0 copy-start.19
  7.2 1.0 copy-start.18
  7.9 18.4 %copy-start.10 = (f32[2,256,1024]{2,1,0:T(8,128)S(1)}, f32[2,256,1024]{2,1,0:T(8,128)}, u32[]{:S(2)}) copy-start(f32[2,256,1024]{2,1,0:T(8,128)} %param.10) | copy-start | bytes 6291460
  9.5 11.1 %all-to-all-start = ((s32[8,2,3]{2,1,0:T(2,128)}), s32[8,2,3]{2,1,0:T(2,128)S(1)}, u32[]{:S(2)}, u32[]{:S(2)}) async-start(s32[8,2,3]{2,1,0:T(2,128)} %bitcast.8), calls=%async_computation | async-start | bytes 16384 | tf_op jit(solution)/shard_map/all_to_all | solution.py:101
  15.3 98.0 %copy-start.13 = (f32[4,128,128]{2,1,0:T(8,128)}, f32[4,128,128]{2,1,0:T(8,128)S(1)}, u32[]{:S(2)}) copy-start(f32[4,128,128]{2,1,0:T(8,128)S(1)} %get-tuple-element.275) | copy-start | bytes 786436
  20.5 121.6 %all-to-all-start.1 = ((f32[8,2,128,128]{3,2,1,0:T(8,128)}), f32[8,2,128,128]{3,2,1,0:T(8,128)}, u32[]{:S(2)}, u32[]{:S(2)}) async-start(f32[8,2,128,128]{3,2,1,0:T(8,128)} %bitcast.24), calls=%async_computation.1 | async-start | bytes 2097152 | tf_op jit(solution)/shard_map/all_to_all | solution.py:102
  26.0 399.8 %all-reduce.15.cloned.1.call-start = ((), (), s32[]{:S(2)}) async-start(), calls=%async_computation.5 | async-start | bytes 1179648 | tf_op jit(solution)/shard_map/psum | solution.py:117
  69.0 1.3 copy-start.5
  113.3 9.4 %copy-start.4 = (f32[16,4,128,128]{3,2,1,0:T(8,128)S(1)}, f32[16,4,128,128]{3,2,1,0:T(8,128)}, u32[]{:S(2)}) copy-start(f32[16,4,128,128]{3,2,1,0:T(8,128)} %fusion.26) | copy-start | bytes 12582916
  122.7 8.9 %copy-start.3 = (f32[16,4,128,128]{3,2,1,0:T(8,128)S(1)}, f32[16,4,128,128]{3,2,1,0:T(8,128)}, u32[]{:S(2)}) copy-start(f32[16,4,128,128]{3,2,1,0:T(8,128)} %fusion.24) | copy-start | bytes 12582916
  129.7 1.9 copy-start
  142.1 3.3 copy-start.2
  152.3 7.0 copy-start.1
  188.1 7.0 copy-start.14
  206.4 2.3 copy-start.6
  208.8 182.6 %copy-start.16 = (f32[4,128,128]{2,1,0:T(8,128)S(1)}, f32[4,128,128]{2,1,0:T(8,128)}, u32[]{:S(2)}) copy-start(f32[4,128,128]{2,1,0:T(8,128)} %get-tuple-element.210) | copy-start | bytes 786436
  387.3 38.8 %copy-start.7 = (f32[2,256,1024]{2,1,0:T(8,128)}, f32[2,256,1024]{2,1,0:T(8,128)S(1)}, u32[]{:S(2)}) copy-start(f32[2,256,1024]{2,1,0:T(8,128)S(1)} %get-tuple-element.506) | copy-start | bytes 6291460
  387.3 4.1 copy-start.17
  392.3 108.7 %all-reduce.11.cloned.1.call-start = ((), (), s32[]{:S(2)}) async-start(), calls=%async_computation.3 | async-start | bytes 1179648 | tf_op jit(solution)/shard_map/psum | solution.py:117
  425.8 236.2 %all-reduce.13.cloned.1.call-start = ((), (), s32[]{:S(2)}) async-start(), calls=%async_computation.4 | async-start | bytes 1179648 | tf_op jit(solution)/shard_map/psum | solution.py:117
  504.3 0.8 copy-start.11
  614.5 12.9 %copy-start.12 = (f32[4,2,128,128]{3,2,1,0:T(8,128)S(1)}, f32[4,2,128,128]{3,2,1,0:T(8,128)}, u32[]{:S(2)}) copy-start(f32[4,2,128,128]{3,2,1,0:T(8,128)} %copy-done.11) | copy-start | bytes 1572868
  626.5 35.6 %copy-start.8 = (f32[2,256,1024]{2,1,0:T(8,128)S(1)}, f32[2,256,1024]{2,1,0:T(8,128)}, u32[]{:S(2)}) copy-start(f32[2,256,1024]{2,1,0:T(8,128)} %copy-done.7) | copy-start | bytes 6291460
  627.4 169.8 %all-reduce.9.cloned.1.call-start = ((), (), s32[]{:S(2)}) async-start(), calls=%async_computation.2 | async-start | bytes 1179648 | tf_op jit(solution)/shard_map/psum | solution.py:117
  797.1 4.1 copy-start.9
Sparse Core Ops, SparseCore 0:
  392.4 33.3 all-reduce.14
  429.2 71.6 all-reduce.10
  627.5 34.5 all-reduce.12
  665.3 71.8 all-reduce.8
